TPU v7x, 32 devices: a whole 2x2x4 slice. The times are simulated.
32 devices in a mesh: box: 4 (over z), row: 4 (over y, core), col: 2 (over x).
Axes of the slice: x: 2, y: 2, z: 4, core: 2. Of those that a mesh axis runs over, the one named last changes fastest.
Arguments:
- ext_ext: float32 [4, 3072, 3072], P('box', 'row', 'col'), may hold values from -6 to 6
- ext_int: float32 [4, 3072, 1024], P('box', 'row', 'col'), may hold values from -0.1875 to 0.1875
- int_ext: float32 [4, 1024, 3072], P('box', 'row', 'col'), may hold values from -6 to 6
- int_int: float32 [4, 1024, 1024], P('box', 'row', 'col'), may hold values from -0.1 to 0.1, as said below
Outputs:
- merged: float32 [4, 3072, 2, 3072], P('box', 'row', None, 'col')
Inputs may be any that keep to these rules, and one draw needn't show every extreme that they name: `int_int`: independent entries.
All inputs are finite; a program needn't handle non-finite values.
Results may differ from a plain program's by a relative error of at most 0.0003.
Values sent between devices are 32-bit elements; how exact they have to be, the bound alone decides.
No kernel may reach another device: no remote copies, remote signals or barrier semaphores. Data moves between devices by JAX's collectives and lax.ppermute only.
A program may use at most 128 MiB of HBM per device.

v0:
```python
import jax
import jax.numpy as jnp
from jax import lax
from jax.sharding import PartitionSpec as P

HIGH = lax.Precision.HIGHEST


def swapped(shard, axis, distance):
    return lax.ppermute(shard, axis, [(i, i ^ 1 << distance) for i in range(lax.axis_size(axis))])


def panel_dot(total, piece, panel):
    return total + jnp.dot(piece, panel, precision=HIGH, preferred_element_type=jnp.float32)


def chain_product(left, right):
    panel = lax.all_gather(right, "row", axis=0, tiled=True)
    empty = jnp.zeros((left.shape[0], right.shape[1]), jnp.float32)
    return panel_dot(empty, lax.all_gather(left, "col", axis=1, tiled=True), panel)


def local(ext_ext, ext_int, int_ext, int_int):
    own_ee = ext_ext[0]
    own_ed = ext_int[0]
    own_de = int_ext[0]
    own_dd = int_int[0]
    partner_dd, partner_de = swapped((own_dd, own_de), "box", 0)
    is_even = lax.axis_index("box") % 2 == 0
    block_rows = own_dd.shape[0]
    block_cols = own_dd.shape[1]
    row_ids = lax.axis_index("row") * block_rows + lax.broadcasted_iota(
        jnp.int32, (block_rows, block_cols), 0
    )
    col_ids = lax.axis_index("col") * block_cols + lax.broadcasted_iota(
        jnp.int32, (block_rows, block_cols), 1
    )
    identity = (row_ids == col_ids).astype(jnp.float32)
    coupling = chain_product(partner_dd, own_dd)
    square = chain_product(coupling, coupling)
    first = identity + coupling
    inverse = first + chain_product(first, square)
    de_panel = lax.all_gather(own_de, "row", axis=0, tiled=True)
    coupled = panel_dot(
        jnp.zeros(own_de.shape, jnp.float32),
        lax.all_gather(partner_dd, "col", axis=1, tiled=True),
        de_panel,
    )
    source = jnp.concatenate(
        [jnp.where(is_even, coupled, partner_de), jnp.where(is_even, partner_de, coupled)], axis=1
    )
    source_panel = lax.all_gather(source, "row", axis=0, tiled=True)
    pieces = lax.all_gather(inverse[None], ("row", "col"), axis=0, tiled=True)
    row_count = lax.axis_size("row")
    col_count = lax.axis_size("col")
    whole = pieces.reshape(row_count, col_count, block_rows, block_cols).transpose(0, 2, 1, 3)
    whole = whole.reshape(row_count * block_rows, col_count * block_cols)
    right_panel = jnp.dot(whole, source_panel, precision=HIGH, preferred_element_type=jnp.float32)
    zeros = jnp.zeros_like(own_ee)
    start_terms = jnp.concatenate(
        [jnp.where(is_even, own_ee, zeros), jnp.where(is_even, zeros, own_ee)], axis=1
    )
    merged = panel_dot(start_terms, lax.all_gather(own_ed, "col", axis=1, tiled=True), right_panel)
    return merged.reshape(1, own_ee.shape[0], 2, own_ee.shape[1])


def solution(mesh):
    placed = (
        P("box", "row", "col"),
        P("box", "row", "col"),
        P("box", "row", "col"),
        P("box", "row", "col"),
    )
    return jax.shard_map(
        local, mesh=mesh, in_specs=placed, out_specs=P("box", "row", None, "col"), check_vma=False
    )
```

profile of v0, /device:TPU:0, one launch (start us, length us, event | category | flops | bytes accessed | tf_op | source)
XLA Modules:
  0.0 469.0 jit_solution(2206762846612566274)
XLA Ops:
  6.5 0.0 all-gather.15.cloned.1.call-start
  6.5 3.1 collective-permute-start
  9.6 12.1 %collective-permute-done = f32[256,512]{1,0:T(8,128)S(1)} collective-permute-done((f32[256,512]{1,0:T(8,128)}, f32[256,512]{1,0:T(8,128)S(1)}, u32[]{:S(2)}, u32[]{:S(2)}) %collective-permute-start) | collective-permute-done | bytes 524320 | tf_op jit(solution)/shard_map/ppermute | solution.py:10
  21.7 0.0 copy-start.2
  21.7 0.8 copy-done.2
  22.5 0.0 all-gather.15.cloned.1.call-update
  22.5 0.0 all-gather.27.cloned.1.call-start
  22.6 0.7 all-gather.27.cloned.1.call-update
  23.3 0.0 all-gather.19.cloned.1.call-start
  23.4 22.0 %all-gather.15.cloned.1.call-done = f32[256,1024]{1,0:T(8,128)} async-done(((f32[256,512]{1,0:T(8,128)}), f32[256,1024]{1,0:T(8,128)}) %all-gather.15.cloned.1.call-update) | async-done | bytes 1048592 | tf_op jit(solution)/shard_map/all_gather | solution.py:20
  45.4 24.2 %all-gather.27.cloned.1.call-done = f32[1,1024,512]{2,1,0:T(8,128)} async-done(((f32[1,256,512]{2,1,0:T(8,128)}), f32[1,1024,512]{2,1,0:T(8,128)}) %all-gather.27.cloned.1.call-update) | async-done | bytes 2097168 | tf_op jit(solution)/shard_map/all_gather | solution.py:18
  69.5 4.8 %convert_add_fusion = (f32[256,512]{1,0:T(8,128)}, f32[256,512]{1,0:T(8,128)}) fusion(s32[512]{0:T(512)S(1)} %iota_add_fusion, s32[256]{0:T(256)S(1)} %iota_add_fusion.1, f32[256,1024]{1,0:T(8,128)} %all-gather.15.cloned.1.call-done, f32[1,1024,512]{2,1,0:T(8,128)} %all-gather.27.cloned.1.call-done), kind=kOutput, calls=%fused_computation.12 | convolution fusion | flops 1611005952 | bytes 4197376 | tf_op jit(solution)/shard_map/dot_general | solution.py:14
  74.4 0.0 copy-start
  74.4 0.0 all-gather.19.cloned.1.call-update
  74.4 0.0 all-gather.21.cloned.1.call-start
  74.4 0.5 all-gather.21.cloned.1.call-update
  75.0 0.0 all-gather.17.cloned.1.call-start
  75.0 0.5 all-gather.17.cloned.1.call-update
  75.6 0.0 all-gather.23.cloned.1.call-start
  75.6 20.2 %all-gather.19.cloned.1.call-done = f32[256,1024]{1,0:T(8,128)} async-done(((f32[256,512]{1,0:T(8,128)}), f32[256,1024]{1,0:T(8,128)}) %all-gather.19.cloned.1.call-update) | async-done | bytes 1048592 | tf_op jit(solution)/shard_map/all_gather | solution.py:20
  95.8 24.0 %all-gather.21.cloned.1.call-done = f32[1024,512]{1,0:T(8,128)} async-done(((f32[256,512]{1,0:T(8,128)}), f32[1024,512]{1,0:T(8,128)}) %all-gather.21.cloned.1.call-update) | async-done | bytes 2097168 | tf_op jit(solution)/shard_map/all_gather | solution.py:18
  119.8 4.6 fusion.5
  124.5 0.0 copy-start.1
  124.5 0.0 all-gather.23.cloned.1.call-update
  124.5 0.0 all-gather.31.cloned.1.call-start
  124.6 0.7 all-gather.31.cloned.1.call-update
  125.3 0.0 all-gather.29.cloned.1.call-start
  125.3 17.2 %all-gather.17.cloned.1.call-done = f32[256,1024]{1,0:T(8,128)} async-done(((f32[256,512]{1,0:T(8,128)}), f32[256,1024]{1,0:T(8,128)}) %all-gather.17.cloned.1.call-update) | async-done | bytes 1048592 | tf_op jit(solution)/shard_map/all_gather | solution.py:20
  142.5 24.0 %all-gather.23.cloned.1.call-done = f32[1024,512]{1,0:T(8,128)} async-done(((f32[256,512]{1,0:T(8,128)}), f32[1024,512]{1,0:T(8,128)}) %all-gather.23.cloned.1.call-update) | async-done | bytes 2097168 | tf_op jit(solution)/shard_map/all_gather | solution.py:18
  166.6 0.0 copy-done
  166.6 4.6 convolution_add_fusion
  171.2 0.0 all-gather.29.cloned.1.call-update
  171.2 0.0 all-gather.25.cloned.1.call-start
  171.3 1.6 collective-permute-start.1
  172.8 35.3 %collective-permute-done.1 = f32[256,1536]{1,0:T(8,128)S(1)} collective-permute-done((f32[256,1536]{1,0:T(8,128)}, f32[256,1536]{1,0:T(8,128)S(1)}, u32[]{:S(2)}, u32[]{:S(2)}) %collective-permute-start.1) | collective-permute-done | bytes 1572896 | tf_op jit(solution)/shard_map/ppermute | solution.py:10
  208.1 6.4 %all-gather.31.cloned.1.call-done = f32[1,1024,1536]{2,1,0:T(8,128)} async-done(((f32[1,256,1536]{2,1,0:T(8,128)}), f32[1,1024,1536]{2,1,0:T(8,128)}) %all-gather.31.cloned.1.call-update) | async-done | bytes 6291472 | tf_op jit(solution)/shard_map/all_gather | solution.py:43
  214.5 0.0 copy-done.1
  214.5 7.6 %broadcast_select_fusion.1 = (f32[256,1536]{1,0:T(8,128)S(1)}, f32[256,1536]{1,0:T(8,128)S(1)}) fusion(f32[256,1536]{1,0:T(8,128)S(1)} %collective-permute-done.1, pred[]{:T(512)S(6)} %eq.8, f32[256,1024]{1,0:T(8,128)S(1)} %copy-done.1, f32[1,1024,1536]{2,1,0:T(8,128)} %all-gather.31.cloned.1.call-done), kind=kOutput, calls=%fused_computation.11 | convolution fusion | flops 4832624640 | bytes 12058625 | tf_op jit(solution)/shard_map/dot_general | solution.py:14
  222.1 1.9 pad_maximum_fusion
  224.1 0.0 all-gather.25.cloned.1.call-update
  224.1 0.2 all-gather.33.cloned.1.call-start
  224.3 0.4 all-gather.33.cloned.1.call-update
  224.7 6.1 %copy.8 = f32[1,768,1536]{1,2,0:T(8,128)} copy(f32[1,768,1536]{2,1,0:T(8,128)} %param.4) | data formatting | bytes 9437184 | tf_op args[0]
  230.7 6.7 %select_bitcast_fusion.1 = (f32[768,1536]{0,1:T(8,128)}, f32[768,1536]{0,1:T(8,128)}) fusion(f32[1,768,1536]{1,2,0:T(8,128)} %copy.8, pred[]{:T(512)S(6)} %eq.8), kind=kLoop, calls=%fused_computation.4 | loop fusion | flops 2359296 | bytes 14155777 | tf_op jit(solution)/shard_map/jit(_where)/select_n | solution.py:61
  237.4 15.6 %all-gather.29.cloned.1.call-done = f32[2048,512]{1,0:T(8,128)} async-done(((f32[256,512]{1,0:T(8,128)}), f32[2048,512]{1,0:T(8,128)}) %all-gather.29.cloned.1.call-update) | async-done | bytes 4194320 | tf_op jit(solution)/shard_map/all_gather | solution.py:53
  253.0 5.4 %copy.10 = f32[4,2,256,512]{3,1,2,0:T(2,128)S(1)} copy(f32[4,2,256,512]{3,2,1,0:T(8,128)} %bitcast.38) | data formatting | bytes 8388608 | tf_op jit(solution)/shard_map/reshape | solution.py:56
  258.4 3.1 copy.12
  261.5 75.2 %all-gather.25.cloned.1.call-done = f32[1024,3072]{1,0:T(8,128)} async-done(((f32[256,3072]{1,0:T(8,128)}), f32[1024,3072]{1,0:T(8,128)}) %all-gather.25.cloned.1.call-update) | async-done | bytes 12582928 | tf_op jit(solution)/shard_map/all_gather | solution.py:52
  336.7 44.8 %fusion.6 = f32[1024,3072]{1,0:T(8,128)} fusion(f32[1024,1024]{1,0:T(8,128)} %bitcast.39, f32[1024,3072]{1,0:T(8,128)} %all-gather.25.cloned.1.call-done), kind=kOutput, calls=%fused_computation.16 | convolution fusion | flops 38654705664 | bytes 29360128 | tf_op jit(solution)/shard_map/dot_general | solution.py:58
  381.4 1.6 all-gather.33.cloned.1.call-done
  383.0 64.4 %maximum_add_fusion = f32[768,3072]{0,1:T(8,128)} fusion(f32[768,1536]{0,1:T(8,128)} %get-tuple-element.6, f32[768,1536]{0,1:T(8,128)} %get-tuple-element.5, f32[1024,3072]{1,0:T(8,128)} %fusion.6, f32[1,768,1024]{2,1,0:T(8,128)} %all-gather.33.cloned.1.call-done), kind=kOutput, calls=%fused_computation | convolution fusion | flops 28995747840 | bytes 34603008 | tf_op jit(solution)/shard_map/dot_general | solution.py:14
  447.4 14.8 %copy.11 = f32[1,768,2,1536]{3,2,1,0:T(2,128)} copy(f32[1,768,2,1536]{1,3,2,0:T(8,128)} %bitcast.37) | data formatting | bytes 18874368 | tf_op jit(solution)/shard_map/reshape | solution.py:64
  (2 shorter events, 0.0 us)
Async XLA Ops:
  6.5 38.9 %all-gather.15.cloned.1.call-start = ((), (), s32[]{:S(2)}) async-start(), calls=%async_computation | async-start | bytes 1572864 | tf_op jit(solution)/shard_map/all_gather | solution.py:20
  6.5 15.2 %collective-permute-start = (f32[256,512]{1,0:T(8,128)}, f32[256,512]{1,0:T(8,128)S(1)}, u32[]{:S(2)}, u32[]{:S(2)}) collective-permute-start(f32[256,512]{1,0:T(8,128)} %bitcast.41), channel_id=1, source_target_pairs={{0,8},{8,0},{16,24},{24,16},{1,9},{9,1},{17,25},{25,17},{2,10},{10... | collective-permute-start | bytes 1572872 | tf_op jit(solution)/shard_map/ppermute | solution.py:10
  21.7 0.8 copy-start.2
  22.5 47.0 %all-gather.27.cloned.1.call-start = ((), (), s32[]{:S(2)}) async-start(), calls=%async_computation.6 | async-start | bytes 2621440 | tf_op jit(solution)/shard_map/all_gather | solution.py:18
  23.3 72.5 %all-gather.19.cloned.1.call-start = ((), (), s32[]{:S(2)}) async-start(), calls=%async_computation.2 | async-start | bytes 1572864 | tf_op jit(solution)/shard_map/all_gather | solution.py:20
  74.4 92.2 %copy-start = (f32[256,512]{1,0:T(8,128)S(1)}, f32[256,512]{1,0:T(8,128)}, u32[]{:S(2)}) copy-start(f32[256,512]{1,0:T(8,128)} %get-tuple-element.9) | copy-start | bytes 1572868
  74.4 45.4 %all-gather.21.cloned.1.call-start = ((), (), s32[]{:S(2)}) async-start(), calls=%async_computation.3 | async-start | bytes 2621440 | tf_op jit(solution)/shard_map/all_gather | solution.py:18
  75.0 67.6 %all-gather.17.cloned.1.call-start = ((), (), s32[]{:S(2)}) async-start(), calls=%async_computation.1 | async-start | bytes 1572864 | tf_op jit(solution)/shard_map/all_gather | solution.py:20
  75.6 91.0 %all-gather.23.cloned.1.call-start = ((), (), s32[]{:S(2)}) async-start(), calls=%async_computation.4 | async-start | bytes 2621440 | tf_op jit(solution)/shard_map/all_gather | solution.py:18
  124.5 90.0 %copy-start.1 = (f32[256,1024]{1,0:T(8,128)S(1)}, f32[256,1024]{1,0:T(8,128)}, u32[]{:S(2)}) copy-start(f32[256,1024]{1,0:T(8,128)} %all-gather.15.cloned.1.call-done) | copy-start | bytes 3145732
  124.5 90.0 %all-gather.31.cloned.1.call-start = ((), (), s32[]{:S(2)}) async-start(), calls=%async_computation.8 | async-start | bytes 7864320 | tf_op jit(solution)/shard_map/all_gather | solution.py:43
  125.3 127.7 %all-gather.29.cloned.1.call-start = ((), (), s32[]{:S(2)}) async-start(), calls=%async_computation.7 | async-start | bytes 4718592 | tf_op jit(solution)/shard_map/all_gather | solution.py:53
  171.2 165.5 %all-gather.25.cloned.1.call-start = ((), (), s32[]{:S(2)}) async-start(), calls=%async_computation.5 | async-start | bytes 15728640 | tf_op jit(solution)/shard_map/all_gather | solution.py:52
  171.3 36.8 %collective-permute-start.1 = (f32[256,1536]{1,0:T(8,128)}, f32[256,1536]{1,0:T(8,128)S(1)}, u32[]{:S(2)}, u32[]{:S(2)}) collective-permute-start(f32[256,1536]{1,0:T(8,128)} %bitcast.40), channel_id=1, source_target_pairs={{0,8},{8,0},{16,24},{24,16},{1,9},{9,1},{17,25},{25,17},{2,10},{10... | collective-permute-start | bytes 4718600 | tf_op jit(solution)/shard_map/ppermute | solution.py:10
  224.1 158.9 %all-gather.33.cloned.1.call-start = ((), (), s32[]{:S(2)}) async-start(), calls=%async_computation.9 | async-start | bytes 4718592 | tf_op jit(solution)/shard_map/all_gather | solution.py:63
Sparse Core Ops, SparseCore 0:
  22.7 22.6 all-gather.14
  46.9 22.5 all-gather.26
  74.5 21.2 all-gather.18
  97.2 22.5 all-gather.20
  121.2 21.2 all-gather.16
  143.9 22.5 all-gather.22
  168.1 46.3 all-gather.30
  216.4 36.5 all-gather.28
  254.6 82.0 all-gather.24
  338.1 44.8 all-gather.32
where the time goes:
time: 470 us; the launch traced here: 469 us
  waiting for transfers between devices  281 us (60%)
  matrix products  131 us (28%)
  local copies, waits for them, and re-layouts  30.1 us (6%)
  between operations  13.6 us (3%)
  other arithmetic  8.65 us (2%)
  starting transfers between devices  5.14 us (1%)
    dot_general x5, matrix products, panel_dot(): jnp.dot(piece, panel, precision=HIGH, preferred_element_type=jnp.float32)  86.1 us
    all_gather x1, waiting for transfers between devices, local(): source_panel = lax.all_gather(source, 'row', axis=0, tiled=True)  75.2 us
    all_gather x3, waiting for transfers between devices, chain_product(): panel = lax.all_gather(right, 'row', axis=0, tiled=True)  72.2 us
    all_gather x3, waiting for transfers between devices, chain_product(): lax.all_gather(left, 'col', axis=1, tiled=True)  59.5 us
    ppermute x2, waiting for transfers between devices, swapped(): lax.ppermute(shard, axis, [(i, i ^ 1 << distance) for i in range(lax.axis...  47.4 us
    dot_general x1, matrix products, local(): jnp.dot(whole, source_panel, precision=HIGH, preferred_element_type=jnp.f...  44.8 us
    all_gather x1, waiting for transfers between devices, local(): pieces = lax.all_gather(inverse[None], ('row', 'col'), axis=0, tiled=True)  15.6 us
    reshape x1, local copies, waits for them, and re-layouts, local(): return merged.reshape(1, own_ee.shape[0], 2, own_ee.shape[1])  14.8 us
  transfers between devices with their start and end apart: 12, of which 12 were waited for; matrix products, arithmetic and copies ran while one was open for 18% of the time, Pallas kernels for 0%

commit v1 on v0

--- a/solution.py
+++ b/solution.py
@@ -4,6 +4,11 @@
 from jax.sharding import PartitionSpec as P
 
 HIGH = lax.Precision.HIGHEST
+
+
+def all_parts(x, axis, along):
+    shards = lax.all_gather(x, axis)
+    return jnp.concatenate(shards, axis=along)
 
 
 def swapped(shard, axis, distance):
@@ -17,7 +22,7 @@
 def chain_product(left, right):
     panel = lax.all_gather(right, "row", axis=0, tiled=True)
     empty = jnp.zeros((left.shape[0], right.shape[1]), jnp.float32)
-    return panel_dot(empty, lax.all_gather(left, "col", axis=1, tiled=True), panel)
+    return panel_dot(empty, all_parts(left, "col", 1), panel)
 
 
 def local(ext_ext, ext_int, int_ext, int_int):

time: 470 us -> 492 us (1.047)
  waiting for transfers between devices: 281 us -> 299 us
    all_gather x1, waiting for transfers between devices: 6.43 us -> 29.8 us  [local(): de_panel = lax.all_gather(own_de, 'row', axis=0, tiled=True)]
    ppermute x2, waiting for transfers between devices: 47.4 us -> 30.3 us  [swapped(): lax.ppermute(shard, axis, [(i, i ^ 1 << distance) for i in range(lax.axis...]
    all_gather x3 -> x4, waiting for transfers between devices: 59.5 us -> 75.8 us  [the longest x3 59 us: all_parts(): shards = lax.all_gather(x, axis)]
  transfers between devices with their start and end apart: 12 -> 13, of which waited for: 12 -> 13; matrix products, arithmetic and copies ran while one was open for 18% -> 18% of each run, Pallas kernels for 0% -> 0%
where the time goes in v1:
time: 492 us; the launch traced here: 491 us
  waiting for transfers between devices  299 us (61%)
  matrix products  130 us (26%)
  local copies, waits for them, and re-layouts  34.8 us (7%)
  between operations  13.3 us (3%)
  other arithmetic  8.65 us (2%)
  starting transfers between devices  5.18 us (1%)
    dot_general x5, matrix products, panel_dot(): jnp.dot(piece, panel, precision=HIGH, preferred_element_type=jnp.float32)  85.5 us
    all_gather x1, waiting for transfers between devices, local(): source_panel = lax.all_gather(source, 'row', axis=0, tiled=True)  75 us
    all_gather x3, waiting for transfers between devices, chain_product(): panel = lax.all_gather(right, 'row', axis=0, tiled=True)  67.5 us
    all_gather x3, waiting for transfers between devices, all_parts(): shards = lax.all_gather(x, axis)  59 us
    dot_general x1, matrix products, local(): jnp.dot(whole, source_panel, precision=HIGH, preferred_element_type=jnp.f...  44.7 us
    ppermute x2, waiting for transfers between devices, swapped(): lax.ppermute(shard, axis, [(i, i ^ 1 << distance) for i in range(lax.axis...  30.3 us
    all_gather x1, waiting for transfers between devices, local(): de_panel = lax.all_gather(own_de, 'row', axis=0, tiled=True)  29.8 us
    all_gather x1, waiting for transfers between devices, local(): lax.all_gather(partner_dd, 'col', axis=1, tiled=True)  16.9 us
  transfers between devices with their start and end apart: 13, of which 13 were waited for; matrix products, arithmetic and copies ran while one was open for 18% of the time, Pallas kernels for 0%

profile of v1, /device:TPU:0, one launch (start us, length us, event | category | flops | bytes accessed | tf_op | source)
XLA Modules:
  0.0 491.2 jit_solution(2488420305270122120)
XLA Ops:
  6.5 0.0 all-gather.27.cloned.1.call-start
  6.5 3.1 collective-permute-start
  9.6 12.1 %collective-permute-done = f32[256,512]{1,0:T(8,128)S(1)} collective-permute-done((f32[256,512]{1,0:T(8,128)}, f32[256,512]{1,0:T(8,128)S(1)}, u32[]{:S(2)}, u32[]{:S(2)}) %collective-permute-start) | collective-permute-done | bytes 524320 | tf_op jit(solution)/shard_map/ppermute | solution.py:15
  21.7 0.0 copy-start.1
  21.7 0.8 copy-done.1
  22.5 0.0 all-gather.27.cloned.1.call-update
  22.5 0.0 all-gather.29.cloned.1.call-start
  22.6 0.7 all-gather.29.cloned.1.call-update
  23.3 0.0 all-gather.33.cloned.1.call-start
  23.4 22.0 %all-gather.27.cloned.1.call-done = f32[512,512]{1,0:T(8,128)} async-done(((f32[256,512]{1,0:T(8,128)}), f32[512,512]{1,0:T(8,128)}) %all-gather.27.cloned.1.call-update) | async-done | bytes 1048592 | tf_op jit(solution)/shard_map/all_gather | solution.py:10
  45.4 1.6 copy.16
  46.9 22.6 %all-gather.29.cloned.1.call-done = f32[1,1024,512]{2,1,0:T(8,128)} async-done(((f32[1,256,512]{2,1,0:T(8,128)}), f32[1,1024,512]{2,1,0:T(8,128)}) %all-gather.29.cloned.1.call-update) | async-done | bytes 2097168 | tf_op jit(solution)/shard_map/all_gather | solution.py:23
  69.5 4.5 convert_add_fusion
  74.0 0.0 all-gather.33.cloned.1.call-update
  74.1 0.0 all-gather.19.cloned.1.call-start
  74.1 0.5 all-gather.19.cloned.1.call-update
  74.7 0.0 all-gather.31.cloned.1.call-start
  74.7 0.5 all-gather.31.cloned.1.call-update
  75.2 0.0 all-gather.21.cloned.1.call-start
  75.3 20.2 %all-gather.33.cloned.1.call-done = f32[512,512]{1,0:T(8,128)} async-done(((f32[256,512]{1,0:T(8,128)}), f32[512,512]{1,0:T(8,128)}) %all-gather.33.cloned.1.call-update) | async-done | bytes 1048592 | tf_op jit(solution)/shard_map/all_gather | solution.py:10
  95.5 1.6 copy.18
  97.1 22.5 %all-gather.19.cloned.1.call-done = f32[1024,512]{1,0:T(8,128)} async-done(((f32[256,512]{1,0:T(8,128)}), f32[1024,512]{1,0:T(8,128)}) %all-gather.19.cloned.1.call-update) | async-done | bytes 2097168 | tf_op jit(solution)/shard_map/all_gather | solution.py:23
  119.5 0.0 copy-start
  119.5 4.4 fusion.5
  123.9 0.0 all-gather.21.cloned.1.call-update
  123.9 0.0 all-gather.23.cloned.1.call-start
  124.0 0.7 all-gather.23.cloned.1.call-update
  124.7 0.0 copy-start.2
  124.7 0.0 all-gather.37.cloned.1.call-start
  124.7 0.7 all-gather.37.cloned.1.call-update
  125.5 0.0 all-gather.35.cloned.1.call-start
  125.5 16.7 %all-gather.31.cloned.1.call-done = f32[512,512]{1,0:T(8,128)} async-done(((f32[256,512]{1,0:T(8,128)}), f32[512,512]{1,0:T(8,128)}) %all-gather.31.cloned.1.call-update) | async-done | bytes 1048592 | tf_op jit(solution)/shard_map/all_gather | solution.py:10
  142.2 1.6 copy.17
  143.8 22.5 %all-gather.21.cloned.1.call-done = f32[1024,512]{1,0:T(8,128)} async-done(((f32[256,512]{1,0:T(8,128)}), f32[1024,512]{1,0:T(8,128)}) %all-gather.21.cloned.1.call-update) | async-done | bytes 2097168 | tf_op jit(solution)/shard_map/all_gather | solution.py:23
  166.2 0.0 copy-done
  166.2 4.3 convolution_add_fusion
  170.6 0.0 all-gather.35.cloned.1.call-update
  170.6 0.0 all-gather.25.cloned.1.call-start
  170.6 0.0 copy-done.2
  170.7 1.5 collective-permute-start.1
  172.2 16.9 %all-gather.23.cloned.1.call-done = f32[256,1024]{1,0:T(8,128)} async-done(((f32[256,512]{1,0:T(8,128)}), f32[256,1024]{1,0:T(8,128)}) %all-gather.23.cloned.1.call-update) | async-done | bytes 1048592 | tf_op jit(solution)/shard_map/all_gather | solution.py:51
  189.1 18.2 %collective-permute-done.1 = f32[256,1536]{1,0:T(8,128)S(1)} collective-permute-done((f32[256,1536]{1,0:T(8,128)S(1)}, f32[256,1536]{1,0:T(8,128)S(1)}, u32[]{:S(2)}, u32[]{:S(2)}) %collective-permute-start.1) | collective-permute-done | bytes 1572896 | tf_op jit(solution)/shard_map/ppermute | solution.py:15
  207.2 29.8 %all-gather.37.cloned.1.call-done = f32[1,1024,1536]{2,1,0:T(8,128)} async-done(((f32[1,256,1536]{2,1,0:T(8,128)}), f32[1,1024,1536]{2,1,0:T(8,128)}) %all-gather.37.cloned.1.call-update) | async-done | bytes 6291472 | tf_op jit(solution)/shard_map/all_gather | solution.py:48
  237.0 7.9 %broadcast_select_fusion.1 = (f32[256,1536]{1,0:T(8,128)S(1)}, f32[256,1536]{1,0:T(8,128)S(1)}) fusion(f32[256,1536]{1,0:T(8,128)S(1)} %collective-permute-done.1, pred[]{:T(512)S(6)} %eq.8, f32[256,1024]{1,0:T(8,128)} %all-gather.23.cloned.1.call-done, f32[1,1024,1536]{2,1,0:T(8,128)} %all-gather.37.cloned.1.call-done), kind=kOutput, calls=%fused_computation.11 | convolution fusion | flops 4832624640 | bytes 12058625 | tf_op jit(solution)/shard_map/dot_general | solution.py:19
  245.0 1.9 pad_maximum_fusion
  246.9 0.0 all-gather.25.cloned.1.call-update
  246.9 0.2 all-gather.39.cloned.1.call-start
  247.1 0.5 all-gather.39.cloned.1.call-update
  247.6 6.0 %copy.14 = f32[1,768,1536]{1,2,0:T(8,128)} copy(f32[1,768,1536]{2,1,0:T(8,128)} %param.4) | data formatting | bytes 9437184 | tf_op args[0]
  253.7 6.7 %select_bitcast_fusion.1 = (f32[768,1536]{0,1:T(8,128)}, f32[768,1536]{0,1:T(8,128)}) fusion(f32[1,768,1536]{1,2,0:T(8,128)} %copy.14, pred[]{:T(512)S(6)} %eq.8), kind=kLoop, calls=%fused_computation.4 | loop fusion | flops 2359296 | bytes 14155777 | tf_op jit(solution)/shard_map/jit(_where)/select_n | solution.py:66
  260.4 15.1 %all-gather.35.cloned.1.call-done = f32[2048,512]{1,0:T(8,128)} async-done(((f32[256,512]{1,0:T(8,128)}), f32[2048,512]{1,0:T(8,128)}) %all-gather.35.cloned.1.call-update) | async-done | bytes 4194320 | tf_op jit(solution)/shard_map/all_gather | solution.py:58
  275.5 5.4 %copy.19 = f32[4,2,256,512]{3,1,2,0:T(2,128)S(1)} copy(f32[4,2,256,512]{3,2,1,0:T(8,128)} %bitcast.51) | data formatting | bytes 8388608 | tf_op jit(solution)/shard_map/reshape | solution.py:61
  281.0 3.1 copy.21
  284.1 75.0 %all-gather.25.cloned.1.call-done = f32[1024,3072]{1,0:T(8,128)} async-done(((f32[256,3072]{1,0:T(8,128)}), f32[1024,3072]{1,0:T(8,128)}) %all-gather.25.cloned.1.call-update) | async-done | bytes 12582928 | tf_op jit(solution)/shard_map/all_gather | solution.py:57
  359.1 44.7 %fusion.6 = f32[1024,3072]{1,0:T(8,128)} fusion(f32[1024,1024]{1,0:T(8,128)} %bitcast.52, f32[1024,3072]{1,0:T(8,128)} %all-gather.25.cloned.1.call-done), kind=kOutput, calls=%fused_computation.16 | convolution fusion | flops 38654705664 | bytes 29360128 | tf_op jit(solution)/shard_map/dot_general | solution.py:63
  403.8 1.7 all-gather.39.cloned.1.call-done
  405.5 64.4 %maximum_add_fusion = f32[768,3072]{0,1:T(8,128)} fusion(f32[768,1536]{0,1:T(8,128)} %get-tuple-element.6, f32[768,1536]{0,1:T(8,128)} %get-tuple-element.5, f32[1024,3072]{1,0:T(8,128)} %fusion.6, f32[1,768,1024]{2,1,0:T(8,128)} %all-gather.39.cloned.1.call-done), kind=kOutput, calls=%fused_computation | convolution fusion | flops 28995747840 | bytes 34603008 | tf_op jit(solution)/shard_map/dot_general | solution.py:19
  469.9 14.8 %copy.20 = f32[1,768,2,1536]{3,2,1,0:T(2,128)} copy(f32[1,768,2,1536]{1,3,2,0:T(8,128)} %bitcast.49) | data formatting | bytes 18874368 | tf_op jit(solution)/shard_map/reshape | solution.py:69
  (2 shorter events, 0.0 us)
Async XLA Ops:
  6.5 38.9 %all-gather.27.cloned.1.call-start = ((), (), s32[]{:S(2)}) async-start(), calls=%async_computation.4 | async-start | bytes 1572864 | tf_op jit(solution)/shard_map/all_gather | solution.py:10
  6.5 15.2 %collective-permute-start = (f32[256,512]{1,0:T(8,128)}, f32[256,512]{1,0:T(8,128)S(1)}, u32[]{:S(2)}, u32[]{:S(2)}) collective-permute-start(f32[256,512]{1,0:T(8,128)} %bitcast.59), channel_id=1, source_target_pairs={{0,8},{8,0},{16,24},{24,16},{1,9},{9,1},{17,25},{25,17},{2,10},{10... | collective-permute-start | bytes 1572872 | tf_op jit(solution)/shard_map/ppermute | solution.py:15
  21.7 0.8 copy-start.1
  22.5 47.0 %all-gather.29.cloned.1.call-start = ((), (), s32[]{:S(2)}) async-start(), calls=%async_computation.5 | async-start | bytes 2621440 | tf_op jit(solution)/shard_map/all_gather | solution.py:23
  23.3 72.2 %all-gather.33.cloned.1.call-start = ((), (), s32[]{:S(2)}) async-start(), calls=%async_computation.7 | async-start | bytes 1572864 | tf_op jit(solution)/shard_map/all_gather | solution.py:10
  74.1 45.4 %all-gather.19.cloned.1.call-start = ((), (), s32[]{:S(2)}) async-start(), calls=%async_computation | async-start | bytes 2621440 | tf_op jit(solution)/shard_map/all_gather | solution.py:23
  74.7 67.6 %all-gather.31.cloned.1.call-start = ((), (), s32[]{:S(2)}) async-start(), calls=%async_computation.6 | async-start | bytes 1572864 | tf_op jit(solution)/shard_map/all_gather | solution.py:10
  75.2 91.0 %all-gather.21.cloned.1.call-start = ((), (), s32[]{:S(2)}) async-start(), calls=%async_computation.1 | async-start | bytes 2621440 | tf_op jit(solution)/shard_map/all_gather | solution.py:23
  119.5 46.7 %copy-start = (f32[256,512]{1,0:T(8,128)S(1)}, f32[256,512]{1,0:T(8,128)}, u32[]{:S(2)}) copy-start(f32[256,512]{1,0:T(8,128)} %get-tuple-element.9) | copy-start | bytes 1572868
  123.9 65.1 %all-gather.23.cloned.1.call-start = ((), (), s32[]{:S(2)}) async-start(), calls=%async_computation.2 | async-start | bytes 1572864 | tf_op jit(solution)/shard_map/all_gather | solution.py:51
  124.7 46.0 %copy-start.2 = (f32[1,256,1536]{2,1,0:T(8,128)S(1)}, f32[1,256,1536]{2,1,0:T(8,128)}, u32[]{:S(2)}) copy-start(f32[1,256,1536]{2,1,0:T(8,128)} %param.6) | copy-start | bytes 4718596
  124.7 112.3 %all-gather.37.cloned.1.call-start = ((), (), s32[]{:S(2)}) async-start(), calls=%async_computation.9 | async-start | bytes 7864320 | tf_op jit(solution)/shard_map/all_gather | solution.py:48
  125.5 150.1 %all-gather.35.cloned.1.call-start = ((), (), s32[]{:S(2)}) async-start(), calls=%async_computation.8 | async-start | bytes 4718592 | tf_op jit(solution)/shard_map/all_gather | solution.py:58
  170.6 188.5 %all-gather.25.cloned.1.call-start = ((), (), s32[]{:S(2)}) async-start(), calls=%async_computation.3 | async-start | bytes 15728640 | tf_op jit(solution)/shard_map/all_gather | solution.py:57
  170.7 36.6 %collective-permute-start.1 = (f32[256,1536]{1,0:T(8,128)S(1)}, f32[256,1536]{1,0:T(8,128)S(1)}, u32[]{:S(2)}, u32[]{:S(2)}) collective-permute-start(f32[256,1536]{1,0:T(8,128)S(1)} %bitcast.55), channel_id=1, source_target_pairs={{0,8},{8,0},{16,24},{24,16},{1,9},{9,1},{17,25},{25,17},{2,10},{10... | collective-permute-start | bytes 4718600 | tf_op jit(solution)/shard_map/ppermute | solution.py:15
  246.9 158.7 %all-gather.39.cloned.1.call-start = ((), (), s32[]{:S(2)}) async-start(), calls=%async_computation.10 | async-start | bytes 4718592 | tf_op jit(solution)/shard_map/all_gather | solution.py:68
Sparse Core Ops, SparseCore 0:
  22.7 22.6 all-gather.26
  46.9 22.5 all-gather.28
  74.2 21.2 all-gather.32
  96.9 22.5 all-gather.18
  120.9 21.2 all-gather.30
  143.6 22.5 all-gather.20
  167.8 21.2 all-gather.22
  190.6 46.3 all-gather.36
  238.9 36.5 all-gather.34
  276.9 82.0 all-gather.24
  360.6 44.8 all-gather.38
